TPU v7x, 128 devices: a whole 4x4x4 slice. The times are simulated.
128 devices in a mesh: gy: 16 (over z_hi, x, core), gz: 8 (over z_lo, y).
Axes of the slice: x: 4, y: 4, z: 4 (z_hi: 2, z_lo: 2; z = z_hi * 2 + z_lo), core: 2. Of those that a mesh axis runs over, the one named last changes fastest.
Arguments:
- reference_image: bfloat16 [64, 1024, 4096], P(None, 'gy', 'gz'), may hold values from -6 to 6
- deformed: bfloat16 [64, 1024, 4096], P(None, 'gy', 'gz'), may hold values from -12 to 12
- displacement: bfloat16 [3, 64, 1024, 4096], P(None, None, 'gy', 'gz'), may hold values from -1 to 1
- plane_factors: float32 [2, 32, 8, 128], P(None, None, None, 'gy'), may hold values from -2.5 to 2.5
- depth_factors: float32 [2, 32, 4096], P(None, None, 'gz'), may hold values from -6 to 6
Outputs:
- residual: bfloat16 [64, 1024, 4096], P(None, 'gy', 'gz')
- step_plane: float32 [2, 32, 8, 128], P(None, None, None, 'gy')
- step_depth: float32 [2, 32, 4096], P(None, None, 'gz')
All inputs are finite; a program needn't handle non-finite values.
Results may differ from a plain program's by a relative error of at most 0.0004.
Values may be sent and summed in bfloat16 or wider, within the bound.
A program may use at most 256 MiB of HBM per device.

v0:
```python
import jax
import jax.numpy as jnp
from jax import lax
from jax.sharding import PartitionSpec as P

RANK = 32
KNOT = 8
epsilon = 1e-06
damping = 0.01
highest = lax.Precision.HIGHEST


def extended(cells, sides, width):
    for axis, dim in sides:
        count = lax.axis_size(axis)
        ends = count - 1
        head = lax.slice_in_dim(cells, 0, width, axis=dim)
        tail = lax.slice_in_dim(cells, cells.shape[dim] - width, cells.shape[dim], axis=dim)
        cells = jnp.concatenate(
            [
                lax.ppermute(tail, axis, [(i, (i + 1) % count) for i in range(ends)]),
                cells,
                lax.ppermute(head, axis, [((i + 1) % count, i) for i in range(ends)]),
            ],
            axis=dim,
        )
    return cells


def tent_weights(shift):
    moved = shift.astype(jnp.float32)
    return [jnp.maximum(0.0, 1.0 - jnp.abs(moved - offset)) for offset in (-1.0, 0.0, 1.0)]


def warp_image(padded, displacement):
    depth_x, width_y, width_z = displacement.shape[1:]
    weight_x = tent_weights(displacement[0])
    weight_y = tent_weights(displacement[1])
    weight_z = tent_weights(displacement[2])
    summed = jnp.zeros((depth_x, width_y, width_z), jnp.float32)
    for along_x in range(3):
        for along_y in range(3):
            partial_z = jnp.zeros((depth_x, width_y, width_z), jnp.float32)
            for along_z in range(3):
                window = padded[
                    along_x : along_x + depth_x,
                    along_y : along_y + width_y,
                    along_z : along_z + width_z,
                ]
                partial_z = partial_z + weight_z[along_z] * window.astype(jnp.float32)
            summed = summed + weight_x[along_x] * weight_y[along_y] * partial_z
    return summed


def expand_nodes(nodes):
    return jnp.repeat(jnp.repeat(nodes, KNOT, axis=2), KNOT, axis=3)


def reduce_nodes(field):
    leading = field.shape[:-2]
    depth_x, width_y = field.shape[-2:]
    shaped = field.reshape(leading + (depth_x // KNOT, KNOT, width_y // KNOT, KNOT))
    return jnp.sum(shaped, axis=(-3, -1))


def contract_rank(left, right):
    return lax.dot_general(left, right, (((0,), (0,)), ((), ())), precision=highest)


def contract_cells(left, right):
    return jnp.dot(left, right, precision=highest)


def contract_depth(left, right):
    return lax.dot_general(left, right, (((1,), (1,)), ((), ())), precision=highest)


def strip_terms(image, padded, displacement, plane_voxels, depth_factors):
    depth_x, width_y, width_z = image.shape
    cells = depth_x * width_y
    warped = warp_image(padded, displacement).reshape(cells, width_z)
    values = image.astype(jnp.float32).reshape(cells, width_z)
    flat_plane = plane_voxels.reshape(2, plane_voxels.shape[1], cells)
    contrast = contract_rank(flat_plane[0], depth_factors[0])
    brightness = contract_rank(flat_plane[1], depth_factors[1])
    misfit = warped - contrast * values - brightness
    product = misfit * values
    squares = values * values
    grad_depth = -jnp.stack(
        [contract_cells(flat_plane[0], product), contract_cells(flat_plane[1], misfit)]
    )
    level_sum = jnp.sum(flat_plane[1] * flat_plane[1], axis=1)
    first_depth = contract_cells(flat_plane[0] * flat_plane[0], squares)
    grad_voxels = -jnp.stack(
        [contract_depth(depth_factors[0], product), contract_depth(depth_factors[1], misfit)]
    )
    diag_voxels = contract_depth(depth_factors[0] * depth_factors[0], squares)
    grad_plane = reduce_nodes(grad_voxels.reshape(2, -1, depth_x, width_y))
    first_diag = reduce_nodes(diag_voxels.reshape(-1, depth_x, width_y))
    depth_level = KNOT * KNOT * jnp.sum(depth_factors[1] * depth_factors[1], axis=1)
    squared_sum = jnp.sum(misfit * misfit)
    residual = misfit.reshape(depth_x, width_y, width_z).astype(jnp.bfloat16)
    return (
        residual,
        squared_sum,
        grad_plane,
        first_diag,
        depth_level,
        grad_depth,
        first_depth,
        level_sum,
    )


def local(reference_image, deformed, displacement, plane_factors, depth_factors):
    rimmed = extended(deformed, (("gy", 1), ("gz", 2)), 1)
    padded = jnp.pad(rimmed, ((1, 1), (0, 0), (0, 0)))
    plane_voxels = expand_nodes(plane_factors)
    (
        residual,
        local_energy,
        grad_plane,
        first_diag,
        depth_level,
        grad_depth,
        first_depth,
        level_sum,
    ) = strip_terms(reference_image, padded, displacement, plane_voxels, depth_factors)
    nodes_x = plane_factors.shape[2]
    nodes_y = plane_factors.shape[3] * lax.axis_size("gy")
    full_z = depth_factors.shape[2] * lax.axis_size("gz")
    energy = lax.psum(local_energy, ("gy", "gz"))
    grad_plane, first_diag, depth_level = lax.psum((grad_plane, first_diag, depth_level), "gz")
    diag_plane = jnp.stack(
        [first_diag, jnp.broadcast_to(depth_level[:, None, None], first_diag.shape)]
    )
    lam_plane = damping * RANK * energy / (nodes_x * nodes_y)
    lam_depth = damping * energy / full_z
    step_plane = -grad_plane / (diag_plane + lam_plane + epsilon)
    grad_depth, first_depth, level_sum = lax.psum((grad_depth, first_depth, level_sum), "gy")
    diag_depth = jnp.stack([first_depth, jnp.broadcast_to(level_sum[:, None], first_depth.shape)])
    step_depth = -grad_depth / (diag_depth + lam_depth + epsilon)
    return (residual, step_plane, step_depth)


def solution(mesh):
    placed = (
        P(None, "gy", "gz"),
        P(None, "gy", "gz"),
        P(None, None, "gy", "gz"),
        P(None, None, None, "gy"),
        P(None, None, "gz"),
    )
    return jax.shard_map(
        local,
        mesh=mesh,
        in_specs=placed,
        out_specs=(P(None, "gy", "gz"), P(None, None, None, "gy"), P(None, None, "gz")),
        check_vma=False,
    )
```

profile of v0, /device:TPU:7, one launch (start us, length us, event | category | flops | bytes accessed | tf_op | source)
XLA Modules:
  0.0 613.2 jit_solution(7184010167852653225)
XLA Ops:
  7.2 0.0 all-reduce.5.cloned.1.call-start
  7.2 1.4 fusion.133
  8.7 6.0 collective-permute-start
  14.7 0.0 copy-start.4
  14.7 2.2 collective-permute-start.1
  16.9 9.0 %fusion.132 = (bf16[1,64,64,512]{3,2,1,0:T(8,128)(2,1)}, bf16[1,64,64,512]{3,2,1,0:T(8,128)(2,1)}, bf16[1,64,64,512]{3,2,1,0:T(8,128)(2,1)}) fusion(bf16[3,64,64,512]{3,2,1,0:T(8,128)(2,1)} %param.7), kind=kLoop, calls=%fused_computation.173 | loop fusion | bytes 25165824 | tf_op jit(solution)/shard_map/slice | solution.py:39
  25.9 0.1 fusion.122
  26.1 0.3 broadcast_in_dim.28
  26.4 8.8 %fusion.124 = f32[4096,512]{1,0:T(8,128)} fusion(f32[32,4096]{0,1:T(8,128)S(1)} %bitcast.293, f32[2,32,512]{2,1,0:T(8,128)S(1)} %copy-done.5), kind=kOutput, calls=%fused_computation.159 | convolution fusion | flops 805306368 | bytes 10551296 | tf_op jit(solution)/shard_map/dot_general | solution.py:67
  35.2 1.2 convert_multiply_fusion
  36.5 7.4 %convolution_reduce_fusion = f32[32,8,8]{0,2,1:T(8,128)} fusion(f32[8,8,8,8,512]{4,3,2,1,0:T(8,128)S(1)} %bitcast.291, f32[2,32,512]{2,1,0:T(8,128)S(1)} %copy-done.5), kind=kOutput, calls=%fused_computation.139 | convolution fusion | flops 805451776 | bytes 8462336 | tf_op jit(solution)/shard_map/dot_general | solution.py:75
  43.9 0.3 broadcast_in_dim.34
  44.2 5.7 convolution_bitcast_fusion.2
  49.8 0.5 broadcast_multiply_fusion
  50.4 13.0 %copy.49 = bf16[64,64,512]{1,0,2:T(8,128)(2,1)} copy(bf16[64,64,512]{2,1,0:T(8,128)(2,1)} %param.6) | data formatting | bytes 8388608 | tf_op args[1]
  63.4 0.2 copy.59
  63.5 12.7 %copy.48 = bf16[64,1,512]{1,0,2:T(8,128)(2,1)} copy(bf16[64,1,512]{2,0,1:T(8,128)(2,1)S(1)} %collective-permute-done) | data formatting | bytes 131072 | tf_op jit(solution)/shard_map/ppermute | solution.py:21
  76.2 12.7 %copy.50 = bf16[64,1,512]{1,0,2:T(8,128)(2,1)} copy(bf16[64,1,512]{2,0,1:T(8,128)(2,1)S(1)} %collective-permute-done.1) | data formatting | bytes 131072 | tf_op jit(solution)/shard_map/ppermute | solution.py:23
  88.9 0.9 pad_maximum_fusion.5
  89.8 3.2 collective-permute-start.2
  93.0 1.3 collective-permute-start.3
  94.3 0.3 broadcast_reduce_fusion
  94.6 13.4 %copy.61 = bf16[1,64,64,512]{2,1,3,0:T(8,128)(2,1)} copy(bf16[1,64,64,512]{3,2,1,0:T(8,128)(2,1)} %get-tuple-element.14) | data formatting | bytes 8388608
  108.0 13.0 %copy.62 = bf16[1,64,64,512]{2,1,3,0:T(8,128)(2,1)} copy(bf16[1,64,64,512]{3,2,1,0:T(8,128)(2,1)} %get-tuple-element.13) | data formatting | bytes 8388608
  121.0 12.9 %copy.63 = bf16[1,64,64,512]{2,1,3,0:T(8,128)(2,1)} copy(bf16[1,64,64,512]{3,2,1,0:T(8,128)(2,1)} %get-tuple-element.12) | data formatting | bytes 8388608
  133.9 32.9 %psum.55 = f32[32]{0:T(128)S(1)} all-reduce(f32[32]{0:T(128)S(1)} %broadcast_reduce_fusion), channel_id=1, replica_groups=mesh['gy'=16,'gz'=8] {'gy'}, use_global_device_ids=true, to_apply=%region_11.12 | all-reduce | flops 32 | bytes 256 | tf_op jit(solution)/shard_map/psum | solution.py:140
  166.8 24.1 %maximum_maximum_fusion = (bf16[64,66,513]{1,0,2:T(8,128)(2,1)S(1)}, bf16[64,66,513]{1,0,2:T(8,128)(2,1)}) fusion(bf16[64,1,512]{1,0,2:T(8,128)(2,1)} %copy.50, bf16[64,64,512]{1,0,2:T(8,128)(2,1)} %copy.49, bf16[64,1,512]{1,0,2:T(8,128)(2,1)} %copy.48, bf16[64,66,1]{1,0,2:T(8,128)(2,1)S(1)} %collective-permute-done.2, ...), kind=kLoop, calls=%fused_computation.126 | loop fusion | flops 34670592 | bytes 13009920 | tf_op jit(solution)/shard_map/concatenate | solution.py:19
  190.8 24.0 %select_maximum_fusion = bf16[66,66,514]{1,0,2:T(8,128)(2,1)S(1)} fusion(bf16[64,66,1]{1,0,2:T(8,128)(2,1)S(1)} %collective-permute-done.3, bf16[64,66,1]{1,0,2:T(8,128)(2,1)S(1)} %collective-permute-done.2, bf16[64,1,512]{1,0,2:T(8,128)(2,1)} %copy.50, bf16[64,64,512]{1,0,2:T(8,128)(2,1)} %copy.49, bf16[64,1,512]{1,0,2:T(8,128)(2,1)} %copy.48), kind=kLoop, calls=%fused_computation.119 | loop fusion | flops 40301712 | bytes 8820240 | tf_op jit(solution)/shard_map/concatenate | solution.py:19
  214.8 119.0 %fusion.15 = f32[64,64,512]{1,0,2:T(8,128)} fusion(bf16[1,64,64,512]{2,1,3,0:T(8,128)(2,1)} %copy.61, bf16[1,64,64,512]{2,1,3,0:T(8,128)(2,1)} %copy.62, bf16[1,64,64,512]{2,1,3,0:T(8,128)(2,1)} %copy.63, bf16[64,64,512]{1,0,2:T(8,128)(2,1)} %copy.49, bf16[66,66,514]{1,0,2:T(8,128)(2,1)S(1)} %select_maximum_fusion, ...), kind=kLoop, calls=%fused_computation.26 | loop fusion | flops 293601280 | bytes 125960192 | tf_op jit(solution)/shard_map/add | solution.py:51
  333.9 12.7 %copy.56 = f32[64,64,512]{2,1,0:T(8,128)} copy(f32[64,64,512]{1,0,2:T(8,128)} %fusion.15) | data formatting | bytes 16777216 | tf_op jit(solution)/shard_map/add | solution.py:51
  346.6 1.6 broadcast_in_dim.32
  348.3 17.3 %multiply_reduce_fusion = (f32[]{:T(128)}, f32[4096,512]{1,0:T(8,128)}, bf16[4096,512]{1,0:T(8,128)(2,1)}, f32[4096,512]{1,0:T(8,128)S(1)}) fusion(bf16[64,64,512]{2,1,0:T(8,128)(2,1)} %param.5, f32[32,4096]{0,1:T(8,128)} %bitcast.295, f32[2,32,512]{2,1,0:T(8,128)S(1)} %copy-done.5, f32[4096,512]{1,0:T(8,128)} %fusion.124, f32[64,64,512]{2,1,0:T(8,128)} %copy.56), kind=kOutput, calls=%fused_computation.135 | convolution fusion | flops 822083584 | bytes 42532868 | tf_op jit(solution)/shard_map/dot_general | solution.py:67
  365.6 10.2 %convolution_bitcast_fusion.4 = f32[1,32,512]{2,1,0:T(8,128)S(1)} fusion(f32[4096,512]{1,0:T(8,128)} %get-tuple-element.16, f32[32,4096]{0,1:T(8,128)S(1)} %bitcast.294), kind=kOutput, calls=%fused_computation.142 | convolution fusion | flops 805306368 | bytes 8978432 | tf_op jit(solution)/shard_map/dot_general | solution.py:71
  375.8 7.7 %convolution_bitcast_fusion.1 = f32[32,4096]{1,0:T(8,128)S(1)} fusion(f32[4096,512]{1,0:T(8,128)S(1)} %copy-done, f32[2,32,512]{2,1,0:T(8,128)S(1)} %copy-done.5), kind=kOutput, calls=%fused_computation.137 | convolution fusion | flops 805306368 | bytes 8978432 | tf_op jit(solution)/shard_map/dot_general | solution.py:75
  383.5 0.0 copy-start.6
  383.6 5.3 convolution_bitcast_fusion.3
  388.8 8.0 %convolution_bitcast_fusion = f32[32,4096]{1,0:T(8,128)S(1)} fusion(f32[4096,512]{1,0:T(8,128)S(1)} %get-tuple-element.22, f32[2,32,512]{2,1,0:T(8,128)S(1)} %copy-done.5), kind=kOutput, calls=%fused_computation.136 | convolution fusion | flops 805306368 | bytes 8978432 | tf_op jit(solution)/shard_map/dot_general | solution.py:75
  396.8 68.7 %psum.52 = f32[]{:T(128)} all-reduce(f32[]{:T(128)} %get-tuple-element.15), channel_id=1, replica_groups=mesh['gy'=16,'gz'=8] {'gy','gz'}, use_global_device_ids=true, to_apply=%region_7.8 | all-reduce | flops 1 | bytes 8 | tf_op jit(solution)/shard_map/psum | solution.py:132
  465.5 0.6 copy.57
  466.1 2.0 copy.58
  468.1 2.2 maximum_reduce_fusion
  471.6 0.7 maximum_negate_fusion
  472.3 0.0 all-reduce.5.cloned.1.call-update
  472.3 26.1 %all-reduce.2 = (f32[32]{0:T(128)S(1)}, f32[1,32,8,8]{1,3,2,0:T(8,128)S(1)}, f32[2,32,8,8]{1,3,2,0:T(8,128)S(1)}) all-reduce(f32[32]{0:T(128)S(1)} %copy-done.8, f32[1,32,8,8]{1,3,2,0:T(8,128)S(1)} %bitcast.303, f32[2,32,8,8]{1,3,2,0:T(8,128)S(1)} %neg.13), channel_id=1, replica_groups=mesh['gy'=16,'gz'=8] {'gz'}, use_global_device_ids=true, to_apply=%region_5.6 | all-reduce | flops 6176 | bytes 49408 | tf_op jit(solution)/shard_map/psum | solution.py:133
  498.4 0.7 fusion.118
  499.1 105.1 %all-reduce.5.cloned.1.call-done = (f32[1,32,512]{2,1,0:T(8,128)}, f32[2,32,512]{2,1,0:T(8,128)}) async-done(((f32[1,32,512]{2,1,0:T(8,128)}, f32[2,32,512]{2,1,0:T(8,128)}), (f32[1,32,512]{2,1,0:T(8,128)}, f32[2,32,512]{2,1,0:T(8,128)})) %all-reduce.5.cloned.1.call-update) | async-done | bytes 196624 | tf_op jit(solution)/shard_map/psum | solution.py:140
  604.2 0.1 stack_broadcast_in_dim.5
  604.2 1.6 fusion.116
  (28 shorter events, 0.2 us)
Async XLA Ops:
  7.2 18.8 %copy-start.7 = (f32[2,32,8,8]{1,3,2,0:T(8,128)S(1)}, f32[2,32,8,8]{1,3,2,0:T(8,128)}, u32[]{:S(2)}) copy-start(f32[2,32,8,8]{1,3,2,0:T(8,128)} %param.8) | copy-start | bytes 49156
  7.2 18.8 %copy-start.5 = (f32[2,32,512]{2,1,0:T(8,128)S(1)}, f32[2,32,512]{2,1,0:T(8,128)}, u32[]{:S(2)}) copy-start(f32[2,32,512]{2,1,0:T(8,128)} %param.9) | copy-start | bytes 393220
  7.2 597.0 %all-reduce.5.cloned.1.call-start = ((), (), s32[]{:S(2)}) async-start(), calls=%async_computation | async-start | bytes 393216 | tf_op jit(solution)/shard_map/psum | solution.py:140
  8.7 54.8 %collective-permute-start = (bf16[64,1,512]{2,0,1:T(8,128)(2,1)S(1)}, bf16[64,1,512]{2,0,1:T(8,128)(2,1)S(1)}, u32[]{:S(2)}, u32[]{:S(2)}) collective-permute-start(bf16[64,1,512]{2,0,1:T(8,128)(2,1)S(1)} %copy.64), channel_id=1, source_target_pairs={{0,8},{8,16},{16,24},{24,32},{32,40},{40,48},{48,56},{56,64},{64,7... | collective-permute-start | bytes 196616 | tf_op jit(solution)/shard_map/ppermute | solution.py:21
  14.7 20.5 %copy-start.4 = (bf16[64,64,512]{2,1,0:T(8,128)(2,1)S(1)}, bf16[64,64,512]{2,1,0:T(8,128)(2,1)}, u32[]{:S(2)}) copy-start(bf16[64,64,512]{2,1,0:T(8,128)(2,1)} %param.5) | copy-start | bytes 12582916
  14.7 61.5 %collective-permute-start.1 = (bf16[64,1,512]{2,0,1:T(8,128)(2,1)S(1)}, bf16[64,1,512]{2,0,1:T(8,128)(2,1)S(1)}, u32[]{:S(2)}, u32[]{:S(2)}) collective-permute-start(bf16[64,1,512]{2,0,1:T(8,128)(2,1)S(1)} %copy.65), channel_id=1, source_target_pairs={{8,0},{16,8},{24,16},{32,24},{40,32},{48,40},{56,48},{64,56},{72,6... | collective-permute-start | bytes 196616 | tf_op jit(solution)/shard_map/ppermute | solution.py:23
  26.4 8.8 %copy-start.1 = (f32[32,64,8,8]{0,3,2,1:T(8,128)}, f32[32,64,8,8]{0,3,2,1:T(8,128)S(1)}, u32[]{:S(2)}) copy-start(f32[32,64,8,8]{0,3,2,1:T(8,128)S(1)} %broadcast_in_dim.28) | copy-start | bytes 1572868
  89.8 77.0 %collective-permute-start.2 = (bf16[64,66,1]{1,0,2:T(8,128)(2,1)S(1)}, bf16[64,66,1]{1,0,2:T(8,128)(2,1)S(1)}, u32[]{:S(2)}, u32[]{:S(2)}) collective-permute-start(bf16[64,66,1]{1,0,2:T(8,128)(2,1)S(1)} %get-tuple-element.10), channel_id=1, source_target_pairs={{0,1},{1,2},{2,3},{3,4},{4,5},{5,6},{6,7},{8,9},{9,10},{10,11},{11... | collective-permute-start | bytes 25352 | tf_op jit(solution)/shard_map/ppermute | solution.py:21
  93.0 73.8 %collective-permute-start.3 = (bf16[64,66,1]{1,0,2:T(8,128)(2,1)S(1)}, bf16[64,66,1]{1,0,2:T(8,128)(2,1)S(1)}, u32[]{:S(2)}, u32[]{:S(2)}) collective-permute-start(bf16[64,66,1]{1,0,2:T(8,128)(2,1)S(1)} %get-tuple-element.11), channel_id=1, source_target_pairs={{1,0},{2,1},{3,2},{4,3},{5,4},{6,5},{7,6},{9,8},{10,9},{11,10},{12... | collective-permute-start | bytes 25352 | tf_op jit(solution)/shard_map/ppermute | solution.py:23
  348.3 17.3 %copy-start.2 = (f32[32,64,8,8]{0,3,2,1:T(8,128)S(1)}, f32[32,64,8,8]{0,3,2,1:T(8,128)}, u32[]{:S(2)}) copy-start(f32[32,64,8,8]{0,3,2,1:T(8,128)} %copy-done.1) | copy-start | bytes 1572868
  365.6 10.2 %copy-start = (f32[4096,512]{1,0:T(8,128)S(1)}, f32[4096,512]{1,0:T(8,128)}, u32[]{:S(2)}) copy-start(f32[4096,512]{1,0:T(8,128)} %get-tuple-element.16) | copy-start | bytes 25165828
  365.6 18.0 %copy-start.3 = (f32[32,64,8,8]{0,3,2,1:T(8,128)S(1)}, f32[32,64,8,8]{0,3,2,1:T(8,128)}, u32[]{:S(2)}) copy-start(f32[32,64,8,8]{0,3,2,1:T(8,128)} %broadcast_in_dim.32) | copy-start | bytes 1572868
  383.5 88.8 %copy-start.6 = (f32[32,8,8]{0,2,1:T(8,128)S(1)}, f32[32,8,8]{0,2,1:T(8,128)}, u32[]{:S(2)}) copy-start(f32[32,8,8]{0,2,1:T(8,128)} %convolution_reduce_fusion) | copy-start | bytes 24580
  383.5 88.8 %copy-start.8 = (f32[32]{0:T(128)S(1)}, f32[32]{0:T(128)}, u32[]{:S(2)}) copy-start(f32[32]{0:T(128)} %broadcast_multiply_fusion) | copy-start | bytes 388
Sparse Core Ops, SparseCore 0:
  472.4 131.7 all-reduce.4
where the time goes:
time: 621 us; the launch traced here: 613 us
  other arithmetic  175 us (28%)
  blocking collectives  128 us (21%)
  local copies, waits for them, and re-layouts  106 us (17%)
  waiting for transfers between devices  105 us (17%)
  matrix products  70.4 us (11%)
  between operations  16.1 us (3%)
  starting transfers between devices  12.7 us (2%)
    add x1, other arithmetic, warp_image(): summed = summed + weight_x[along_x] * weight_y[along_y] * partial_z  119 us
    psum x1, waiting for transfers between devices, local(): lax.psum((grad_depth, first_depth, level_sum), 'gy')  105 us
    psum x1, blocking collectives, local(): energy = lax.psum(local_energy, ('gy', 'gz'))  68.7 us
    unnamed x24, local copies, waits for them, and re-layouts  52.3 us
    concatenate x2, other arithmetic, extended(): jnp.concatenate([lax.ppermute(tail, axis, [(i, (i + 1) % count) for i in...  48.1 us
    psum x1, blocking collectives, local(): lax.psum((grad_depth, first_depth, level_sum), 'gy')  32.9 us
    psum x1, blocking collectives, local(): lax.psum((grad_plane, first_diag, depth_level), 'gz')  26.1 us
    dot_general x2, matrix products, contract_rank(): lax.dot_general(left, right, (((0,), (0,)), ((), ())), precision=highest)  26.1 us
  transfers between devices with their start and end apart: 5, of which 1 were waited for; matrix products, arithmetic and copies ran while one was open for 16% of the time, Pallas kernels for 0%

commit v1 on v0

--- a/solution.py
+++ b/solution.py
@@ -129,7 +129,7 @@
     nodes_x = plane_factors.shape[2]
     nodes_y = plane_factors.shape[3] * lax.axis_size("gy")
     full_z = depth_factors.shape[2] * lax.axis_size("gz")
-    energy = lax.psum(local_energy, ("gy", "gz"))
+    energy = lax.psum(lax.psum(local_energy, "gz"), "gy")
     grad_plane, first_diag, depth_level = lax.psum((grad_plane, first_diag, depth_level), "gz")
     diag_plane = jnp.stack(
         [first_diag, jnp.broadcast_to(depth_level[:, None, None], first_diag.shape)]

time: 621 us -> 591 us (0.952)
  blocking collectives: 128 us -> 70.5 us
  waiting for transfers between devices: 105 us -> 132 us
    psum x2 -> x1, blocking collectives: 102 us -> 41.7 us  [local(): energy = lax.psum(lax.psum(local_energy, 'gz'), 'gy')]
    psum x1, waiting for transfers between devices: 105 us -> 132 us  [local(): lax.psum((grad_depth, first_depth, level_sum), 'gy')]
  transfers between devices with their start and end apart: 5 -> 5, of which waited for: 1 -> 1; matrix products, arithmetic and copies ran while one was open for 16% -> 17% of each run, Pallas kernels for 0% -> 0%
where the time goes in v1:
time: 591 us; the launch traced here: 583 us
  other arithmetic  176 us (30%)
  waiting for transfers between devices  132 us (22%)
  local copies, waits for them, and re-layouts  106 us (18%)
  matrix products  70.8 us (12%)
  blocking collectives  70.5 us (12%)
  between operations  15.9 us (3%)
  starting transfers between devices  12.7 us (2%)
    psum x1, waiting for transfers between devices, local(): lax.psum((grad_depth, first_depth, level_sum), 'gy')  132 us
    add x1, other arithmetic, warp_image(): summed = summed + weight_x[along_x] * weight_y[along_y] * partial_z  119 us
    unnamed x24, local copies, waits for them, and re-layouts  52.1 us
    concatenate x2, other arithmetic, extended(): jnp.concatenate([lax.ppermute(tail, axis, [(i, (i + 1) % count) for i in...  48.3 us
    psum x1, blocking collectives, local(): energy = lax.psum(lax.psum(local_energy, 'gz'), 'gy')  41.7 us
    psum x1, blocking collectives, local(): lax.psum((grad_plane, first_diag, depth_level), 'gz')  28.8 us
    dot_general x2, matrix products, contract_rank(): lax.dot_general(left, right, (((0,), (0,)), ((), ())), precision=highest)  26.5 us
    dot_general x3, matrix products, contract_depth(): lax.dot_general(left, right, (((1,), (1,)), ((), ())), precision=highest)  23.1 us
  transfers between devices with their start and end apart: 5, of which 1 were waited for; matrix products, arithmetic and copies ran while one was open for 17% of the time, Pallas kernels for 0%

profile of v1, /device:TPU:7, one launch (start us, length us, event | category | flops | bytes accessed | tf_op | source)
XLA Modules:
  0.0 583.4 jit_solution(7792110212231260446)
XLA Ops:
  7.2 0.0 all-reduce.6.cloned.1.call-start
  7.2 1.4 fusion.133
  8.7 6.0 %collective-permute-start = (bf16[64,1,512]{2,0,1:T(8,128)(2,1)S(1)}, bf16[64,1,512]{2,0,1:T(8,128)(2,1)S(1)}, u32[]{:S(2)}, u32[]{:S(2)}) collective-permute-start(bf16[64,1,512]{2,0,1:T(8,128)(2,1)S(1)} %copy.64), channel_id=1, source_target_pairs={{0,8},{8,16},{16,24},{24,32},{32,40},{40,48},{48,56},{56,64},{64,7... | collective-permute-start | bytes 196616 | tf_op jit(solution)/shard_map/ppermute | solution.py:21
  14.7 0.0 copy-start.4
  14.7 2.2 collective-permute-start.1
  16.9 9.0 %fusion.132 = (bf16[1,64,64,512]{3,2,1,0:T(8,128)(2,1)}, bf16[1,64,64,512]{3,2,1,0:T(8,128)(2,1)}, bf16[1,64,64,512]{3,2,1,0:T(8,128)(2,1)}) fusion(bf16[3,64,64,512]{3,2,1,0:T(8,128)(2,1)} %param.7), kind=kLoop, calls=%fused_computation.173 | loop fusion | bytes 25165824 | tf_op jit(solution)/shard_map/slice | solution.py:39
  25.9 0.1 fusion.122
  26.1 0.3 broadcast_in_dim.28
  26.4 8.8 %fusion.124 = f32[4096,512]{1,0:T(8,128)} fusion(f32[32,4096]{0,1:T(8,128)S(1)} %bitcast.293, f32[2,32,512]{2,1,0:T(8,128)S(1)} %copy-done.5), kind=kOutput, calls=%fused_computation.159 | convolution fusion | flops 805306368 | bytes 10551296 | tf_op jit(solution)/shard_map/dot_general | solution.py:67
  35.2 1.2 convert_multiply_fusion
  36.4 7.5 %convolution_reduce_fusion = f32[32,8,8]{0,2,1:T(8,128)} fusion(f32[8,8,8,8,512]{4,3,2,1,0:T(8,128)S(1)} %bitcast.291, f32[2,32,512]{2,1,0:T(8,128)S(1)} %copy-done.5), kind=kOutput, calls=%fused_computation.139 | convolution fusion | flops 805451776 | bytes 8462336 | tf_op jit(solution)/shard_map/dot_general | solution.py:75
  43.9 0.3 broadcast_in_dim.34
  44.2 5.7 convolution_bitcast_fusion.2
  49.9 0.6 broadcast_multiply_fusion
  50.4 13.0 %copy.49 = bf16[64,64,512]{1,0,2:T(8,128)(2,1)} copy(bf16[64,64,512]{2,1,0:T(8,128)(2,1)} %param.6) | data formatting | bytes 8388608 | tf_op args[1]
  63.4 0.2 copy.59
  63.6 0.0 collective-permute-done
  63.6 12.7 %copy.48 = bf16[64,1,512]{1,0,2:T(8,128)(2,1)} copy(bf16[64,1,512]{2,0,1:T(8,128)(2,1)S(1)} %collective-permute-done) | data formatting | bytes 131072 | tf_op jit(solution)/shard_map/ppermute | solution.py:21
  76.2 12.7 %copy.50 = bf16[64,1,512]{1,0,2:T(8,128)(2,1)} copy(bf16[64,1,512]{2,0,1:T(8,128)(2,1)S(1)} %collective-permute-done.1) | data formatting | bytes 131072 | tf_op jit(solution)/shard_map/ppermute | solution.py:23
  88.9 0.9 pad_maximum_fusion.5
  89.8 3.2 collective-permute-start.2
  93.0 1.3 collective-permute-start.3
  94.3 0.3 broadcast_reduce_fusion
  94.7 13.2 %copy.61 = bf16[1,64,64,512]{2,1,3,0:T(8,128)(2,1)} copy(bf16[1,64,64,512]{3,2,1,0:T(8,128)(2,1)} %get-tuple-element.17) | data formatting | bytes 8388608
  107.8 13.0 %copy.62 = bf16[1,64,64,512]{2,1,3,0:T(8,128)(2,1)} copy(bf16[1,64,64,512]{3,2,1,0:T(8,128)(2,1)} %get-tuple-element.16) | data formatting | bytes 8388608
  120.8 12.9 %copy.63 = bf16[1,64,64,512]{2,1,3,0:T(8,128)(2,1)} copy(bf16[1,64,64,512]{3,2,1,0:T(8,128)(2,1)} %get-tuple-element.15) | data formatting | bytes 8388608
  133.7 24.1 %maximum_maximum_fusion = (bf16[64,66,513]{1,0,2:T(8,128)(2,1)S(1)}, bf16[64,66,513]{1,0,2:T(8,128)(2,1)}) fusion(bf16[64,1,512]{1,0,2:T(8,128)(2,1)} %copy.50, bf16[64,64,512]{1,0,2:T(8,128)(2,1)} %copy.49, bf16[64,1,512]{1,0,2:T(8,128)(2,1)} %copy.48, bf16[64,66,1]{1,0,2:T(8,128)(2,1)S(1)} %collective-permute-done.2, ...), kind=kLoop, calls=%fused_computation.126 | loop fusion | flops 34670592 | bytes 13009920 | tf_op jit(solution)/shard_map/concatenate | solution.py:19
  157.8 24.2 %select_maximum_fusion = bf16[66,66,514]{1,0,2:T(8,128)(2,1)S(1)} fusion(bf16[64,66,1]{1,0,2:T(8,128)(2,1)S(1)} %collective-permute-done.3, bf16[64,66,1]{1,0,2:T(8,128)(2,1)S(1)} %collective-permute-done.2, bf16[64,1,512]{1,0,2:T(8,128)(2,1)} %copy.50, bf16[64,64,512]{1,0,2:T(8,128)(2,1)} %copy.49, bf16[64,1,512]{1,0,2:T(8,128)(2,1)} %copy.48), kind=kLoop, calls=%fused_computation.119 | loop fusion | flops 40301712 | bytes 8820240 | tf_op jit(solution)/shard_map/concatenate | solution.py:19
  182.1 118.9 %fusion.15 = f32[64,64,512]{1,0,2:T(8,128)} fusion(bf16[1,64,64,512]{2,1,3,0:T(8,128)(2,1)} %copy.61, bf16[1,64,64,512]{2,1,3,0:T(8,128)(2,1)} %copy.62, bf16[1,64,64,512]{2,1,3,0:T(8,128)(2,1)} %copy.63, bf16[64,64,512]{1,0,2:T(8,128)(2,1)} %copy.49, bf16[66,66,514]{1,0,2:T(8,128)(2,1)S(1)} %select_maximum_fusion, ...), kind=kLoop, calls=%fused_computation.26 | loop fusion | flops 293601280 | bytes 125960192 | tf_op jit(solution)/shard_map/add | solution.py:51
  301.0 12.7 %copy.56 = f32[64,64,512]{2,1,0:T(8,128)} copy(f32[64,64,512]{1,0,2:T(8,128)} %fusion.15) | data formatting | bytes 16777216 | tf_op jit(solution)/shard_map/add | solution.py:51
  313.8 1.6 broadcast_in_dim.32
  315.4 17.8 %multiply_reduce_fusion = (f32[]{:T(128)}, f32[4096,512]{1,0:T(8,128)}, bf16[4096,512]{1,0:T(8,128)(2,1)}, f32[4096,512]{1,0:T(8,128)S(1)}) fusion(bf16[64,64,512]{2,1,0:T(8,128)(2,1)} %param.5, f32[32,4096]{0,1:T(8,128)} %bitcast.295, f32[2,32,512]{2,1,0:T(8,128)S(1)} %copy-done.5, f32[4096,512]{1,0:T(8,128)} %fusion.124, f32[64,64,512]{2,1,0:T(8,128)} %copy.56), kind=kOutput, calls=%fused_computation.135 | convolution fusion | flops 822083584 | bytes 42532868 | tf_op jit(solution)/shard_map/dot_general | solution.py:67
  333.2 10.2 %convolution_bitcast_fusion.4 = f32[1,32,512]{2,1,0:T(8,128)S(1)} fusion(f32[4096,512]{1,0:T(8,128)} %get-tuple-element.19, f32[32,4096]{0,1:T(8,128)S(1)} %bitcast.294), kind=kOutput, calls=%fused_computation.142 | convolution fusion | flops 805306368 | bytes 8978432 | tf_op jit(solution)/shard_map/dot_general | solution.py:71
  343.3 7.7 %convolution_bitcast_fusion.1 = f32[32,4096]{1,0:T(8,128)S(1)} fusion(f32[4096,512]{1,0:T(8,128)S(1)} %copy-done, f32[2,32,512]{2,1,0:T(8,128)S(1)} %copy-done.5), kind=kOutput, calls=%fused_computation.137 | convolution fusion | flops 805306368 | bytes 8978432 | tf_op jit(solution)/shard_map/dot_general | solution.py:75
  351.1 0.0 copy-start.6
  351.1 5.3 convolution_bitcast_fusion.3
  356.4 7.9 %convolution_bitcast_fusion = f32[32,4096]{1,0:T(8,128)S(1)} fusion(f32[4096,512]{1,0:T(8,128)S(1)} %get-tuple-element.25, f32[2,32,512]{2,1,0:T(8,128)S(1)} %copy-done.5), kind=kOutput, calls=%fused_computation.136 | convolution fusion | flops 805306368 | bytes 8978432 | tf_op jit(solution)/shard_map/dot_general | solution.py:75
  364.3 0.6 copy.57
  364.9 1.9 copy.58
  366.9 2.2 maximum_reduce_fusion
  369.1 28.8 %all-reduce.3 = (f32[32]{0:T(128)S(1)}, f32[1,32,8,8]{1,3,2,0:T(8,128)S(1)}, f32[2,32,8,8]{1,3,2,0:T(8,128)S(1)}, f32[]{:T(128)}) all-reduce(f32[32]{0:T(128)S(1)} %copy-done.8, f32[1,32,8,8]{1,3,2,0:T(8,128)S(1)} %bitcast.303, f32[2,32,8,8]{1,3,2,0:T(8,128)S(1)} %neg.13, f32[]{:T(128)} %get-tuple-element.18), channel_id=1, replica_groups=mesh['gy'=16,'gz'=8] {'gz'}, use_global_device_ids=true, to_apply=%region_5.6 | all-reduce | flops 6177 | bytes 49416 | tf_op jit(solution)/shard_map/psum | solution.py:133
  398.0 41.7 %all-reduce.1 = (f32[]{:T(128)}, f32[32]{0:T(128)S(1)}) all-reduce(f32[]{:T(128)} %get-tuple-element.10, f32[32]{0:T(128)S(1)} %broadcast_reduce_fusion), channel_id=1, replica_groups=mesh['gy'=16,'gz'=8] {'gy'}, use_global_device_ids=true, to_apply=%region_8.9 | all-reduce | flops 33 | bytes 264 | tf_op jit(solution)/shard_map/psum | solution.py:132
  440.9 0.7 maximum_negate_fusion
  441.6 0.0 all-reduce.6.cloned.1.call-update
  441.6 0.7 fusion.118
  442.3 132.4 %all-reduce.6.cloned.1.call-done = (f32[1,32,512]{2,1,0:T(8,128)}, f32[2,32,512]{2,1,0:T(8,128)}) async-done(((f32[1,32,512]{2,1,0:T(8,128)}, f32[2,32,512]{2,1,0:T(8,128)}), (f32[1,32,512]{2,1,0:T(8,128)}, f32[2,32,512]{2,1,0:T(8,128)})) %all-reduce.6.cloned.1.call-update) | async-done | bytes 196624 | tf_op jit(solution)/shard_map/psum | solution.py:140
  574.7 0.1 stack_broadcast_in_dim.5
  574.7 1.6 fusion.116
  (27 shorter events, 0.2 us)
Async XLA Ops:
  7.2 18.8 %copy-start.7 = (f32[2,32,8,8]{1,3,2,0:T(8,128)S(1)}, f32[2,32,8,8]{1,3,2,0:T(8,128)}, u32[]{:S(2)}) copy-start(f32[2,32,8,8]{1,3,2,0:T(8,128)} %param.8) | copy-start | bytes 49156
  7.2 18.8 %copy-start.5 = (f32[2,32,512]{2,1,0:T(8,128)S(1)}, f32[2,32,512]{2,1,0:T(8,128)}, u32[]{:S(2)}) copy-start(f32[2,32,512]{2,1,0:T(8,128)} %param.9) | copy-start | bytes 393220
  7.2 567.5 %all-reduce.6.cloned.1.call-start = ((), (), s32[]{:S(2)}) async-start(), calls=%async_computation | async-start | bytes 393216 | tf_op jit(solution)/shard_map/psum | solution.py:140
  8.7 54.9 %collective-permute-start = (bf16[64,1,512]{2,0,1:T(8,128)(2,1)S(1)}, bf16[64,1,512]{2,0,1:T(8,128)(2,1)S(1)}, u32[]{:S(2)}, u32[]{:S(2)}) collective-permute-start(bf16[64,1,512]{2,0,1:T(8,128)(2,1)S(1)} %copy.64), channel_id=1, source_target_pairs={{0,8},{8,16},{16,24},{24,32},{32,40},{40,48},{48,56},{56,64},{64,7... | collective-permute-start | bytes 196616 | tf_op jit(solution)/shard_map/ppermute | solution.py:21
  14.7 20.5 %copy-start.4 = (bf16[64,64,512]{2,1,0:T(8,128)(2,1)S(1)}, bf16[64,64,512]{2,1,0:T(8,128)(2,1)}, u32[]{:S(2)}) copy-start(bf16[64,64,512]{2,1,0:T(8,128)(2,1)} %param.5) | copy-start | bytes 12582916
  14.7 61.5 %collective-permute-start.1 = (bf16[64,1,512]{2,0,1:T(8,128)(2,1)S(1)}, bf16[64,1,512]{2,0,1:T(8,128)(2,1)S(1)}, u32[]{:S(2)}, u32[]{:S(2)}) collective-permute-start(bf16[64,1,512]{2,0,1:T(8,128)(2,1)S(1)} %copy.65), channel_id=1, source_target_pairs={{8,0},{16,8},{24,16},{32,24},{40,32},{48,40},{56,48},{64,56},{72,6... | collective-permute-start | bytes 196616 | tf_op jit(solution)/shard_map/ppermute | solution.py:23
  26.4 8.8 %copy-start.1 = (f32[32,64,8,8]{0,3,2,1:T(8,128)}, f32[32,64,8,8]{0,3,2,1:T(8,128)S(1)}, u32[]{:S(2)}) copy-start(f32[32,64,8,8]{0,3,2,1:T(8,128)S(1)} %broadcast_in_dim.28) | copy-start | bytes 1572868
  89.8 43.9 %collective-permute-start.2 = (bf16[64,66,1]{1,0,2:T(8,128)(2,1)S(1)}, bf16[64,66,1]{1,0,2:T(8,128)(2,1)S(1)}, u32[]{:S(2)}, u32[]{:S(2)}) collective-permute-start(bf16[64,66,1]{1,0,2:T(8,128)(2,1)S(1)} %get-tuple-element.13), channel_id=1, source_target_pairs={{0,1},{1,2},{2,3},{3,4},{4,5},{5,6},{6,7},{8,9},{9,10},{10,11},{11... | collective-permute-start | bytes 25352 | tf_op jit(solution)/shard_map/ppermute | solution.py:21
  93.0 40.7 %collective-permute-start.3 = (bf16[64,66,1]{1,0,2:T(8,128)(2,1)S(1)}, bf16[64,66,1]{1,0,2:T(8,128)(2,1)S(1)}, u32[]{:S(2)}, u32[]{:S(2)}) collective-permute-start(bf16[64,66,1]{1,0,2:T(8,128)(2,1)S(1)} %get-tuple-element.14), channel_id=1, source_target_pairs={{1,0},{2,1},{3,2},{4,3},{5,4},{6,5},{7,6},{9,8},{10,9},{11,10},{12... | collective-permute-start | bytes 25352 | tf_op jit(solution)/shard_map/ppermute | solution.py:23
  315.4 17.8 %copy-start.2 = (f32[32,64,8,8]{0,3,2,1:T(8,128)S(1)}, f32[32,64,8,8]{0,3,2,1:T(8,128)}, u32[]{:S(2)}) copy-start(f32[32,64,8,8]{0,3,2,1:T(8,128)} %copy-done.1) | copy-start | bytes 1572868
  333.2 10.2 %copy-start = (f32[4096,512]{1,0:T(8,128)S(1)}, f32[4096,512]{1,0:T(8,128)}, u32[]{:S(2)}) copy-start(f32[4096,512]{1,0:T(8,128)} %get-tuple-element.19) | copy-start | bytes 25165828
  333.2 17.9 %copy-start.3 = (f32[32,64,8,8]{0,3,2,1:T(8,128)S(1)}, f32[32,64,8,8]{0,3,2,1:T(8,128)}, u32[]{:S(2)}) copy-start(f32[32,64,8,8]{0,3,2,1:T(8,128)} %broadcast_in_dim.32) | copy-start | bytes 1572868
  351.1 18.0 %copy-start.6 = (f32[32,8,8]{0,2,1:T(8,128)S(1)}, f32[32,8,8]{0,2,1:T(8,128)}, u32[]{:S(2)}) copy-start(f32[32,8,8]{0,2,1:T(8,128)} %convolution_reduce_fusion) | copy-start | bytes 24580
  351.1 18.0 %copy-start.8 = (f32[32]{0:T(128)S(1)}, f32[32]{0:T(128)}, u32[]{:S(2)}) copy-start(f32[32]{0:T(128)} %broadcast_multiply_fusion) | copy-start | bytes 388
Sparse Core Ops, SparseCore 0:
  441.7 132.8 all-reduce.5
